TPU v7x, 32 devices: a whole 2x2x4 slice. The times are simulated.
32 devices in a mesh: dp: 8 (over y, x, core), mp: 4 (over z).
Axes of the slice: x: 2, y: 2, z: 4, core: 2. Of those that a mesh axis runs over, the one named last changes fastest.
Arguments:
- pooled: bfloat16 [2048, 3584], P('dp', 'mp'), may hold values from -4 to 4
- w_out: bfloat16 [3584, 3584], P('mp'), may hold values from -0.028931878 to 0.028931878
- assignments: int32 [2048], P('dp'), may hold values from 0 to 4095
- ema_sums: float32 [4096, 3584], P('mp', 'dp'), may hold values from -0.40089186 to 0.40089186
- ema_counts: float32 [4096], P('mp'), may hold values from 1 to 8
Outputs:
- distances: float32 [2048, 4096], P('dp', 'mp')
- new_sums: float32 [4096, 3584], P('mp', 'dp')
- new_counts: float32 [4096], P('mp')
- new_centroids: bfloat16 [4096, 3584], P('mp', 'dp')
All inputs are finite; a program needn't handle non-finite values.
Results may differ from a plain program's by a relative error of at most 0.0011.
Values may be sent and summed in bfloat16 or wider, within the bound.
A program may use at most 64 MiB of HBM per device.

v0:
```python
import math
import jax
import jax.numpy as jnp
from jax import lax
from jax.sharding import PartitionSpec as P

EPSILON = 1e-06
EMA_DECAY = 0.9


def body(pooled, w_out, assignments, ema_sums, ema_counts):
    partial_value = jnp.dot(pooled, w_out, preferred_element_type=jnp.float32)
    projected = lax.psum(partial_value, "mp")
    inverse_norm = 1.0 / jnp.sqrt(jnp.sum(projected * projected, axis=1, keepdims=True) + EPSILON)
    embedded = (projected * inverse_norm).astype(jnp.bfloat16)
    local_centers = ema_sums.shape[0]
    doc_rows = embedded.shape[0]
    centers = (ema_sums / ema_counts[:, None]).astype(jnp.bfloat16)
    column_piece = lax.all_gather(centers, "dp", axis=1, tiled=True)
    products = lax.dot_general(
        embedded, column_piece, (((1,), (1,)), ((), ())), preferred_element_type=jnp.float32
    )
    piece_wide = column_piece.astype(jnp.float32)
    center_norms = jnp.sum(piece_wide * piece_wide, axis=1)
    products, center_norms = (products, center_norms)
    embed_wide = embedded.astype(jnp.float32)
    doc_norms = jnp.sum(embed_wide * embed_wide, axis=1)
    distances = doc_norms[:, None] + center_norms[None, :] - 2.0 * products
    first_center = lax.axis_index("mp") * local_centers
    center_ids = first_center + jnp.arange(local_centers, dtype=jnp.int32)
    feature_cols = ema_sums.shape[1]
    every_assign = lax.all_gather(assignments, "dp", axis=0, tiled=True)
    own_columns = lax.all_to_all(embedded, "dp", split_axis=1, concat_axis=0, tiled=True)
    shard_count = lax.axis_size("dp")
    group_size = math.gcd(shard_count, max(1, 2048 // doc_rows))
    block_rows = group_size * doc_rows
    turns = shard_count // group_size

    def add_block(block_index, totals):
        sums_now, counts_now = totals
        block_assign = lax.dynamic_slice_in_dim(
            every_assign, block_index * block_rows, block_rows, 0
        )
        block_columns = lax.dynamic_slice_in_dim(
            own_columns, block_index * block_rows, block_rows, 0
        )
        one_hot = (block_assign[None, :] == center_ids[:, None]).astype(jnp.bfloat16)
        sums_now = sums_now + jnp.dot(one_hot, block_columns, preferred_element_type=jnp.float32)
        counts_now = counts_now + jnp.sum(one_hot, axis=1, dtype=jnp.float32)
        return (sums_now, counts_now)

    start_sums = (
        jnp.zeros((local_centers, feature_cols), jnp.float32),
        jnp.zeros((local_centers,), jnp.float32),
    )
    batch_sums, batch_counts = lax.fori_loop(0, turns, add_block, start_sums)
    new_counts = EMA_DECAY * ema_counts + (1.0 - EMA_DECAY) * batch_counts
    new_sums = EMA_DECAY * ema_sums + (1.0 - EMA_DECAY) * batch_sums
    new_centroids = (new_sums / new_counts[:, None]).astype(jnp.bfloat16)
    return (distances, new_sums, new_counts, new_centroids)


def solution(mesh):
    return jax.shard_map(
        body,
        mesh=mesh,
        in_specs=(P("dp", "mp"), P("mp", None), P("dp"), P("mp", "dp"), P("mp")),
        out_specs=(P("dp", "mp"), P("mp", "dp"), P("mp"), P("mp", "dp")),
        check_vma=False,
    )
```

profile of v0, /device:TPU:0, one launch (start us, length us, event | category | flops | bytes accessed | tf_op | source)
XLA Modules:
  0.0 215.6 jit_solution(4043559094026590558)
XLA Ops:
  8.0 0.0 copy-start
  8.0 0.0 all-reduce.2.cloned.1.call-start
  8.1 1.0 copy-done
  9.0 6.8 %fusion.7 = f32[256,3584]{1,0:T(8,128)} fusion(bf16[256,896]{1,0:T(8,128)(2,1)S(1)} %copy-done, bf16[896,3584]{1,0:T(8,128)(2,1)} %param.6), kind=kOutput, calls=%fused_computation.18 | convolution fusion | flops 1644167168 | bytes 10551296 | tf_op jit(solution)/shard_map/dot_general | solution.py:12
  15.8 0.0 all-reduce.2.cloned.1.call-update
  15.8 0.0 all-gather.3.cloned.1.call-start
  15.9 1.4 copy-done.5
  17.3 1.1 divide_convert_fusion.1
  18.5 0.0 all-gather.3.cloned.1.call-update
  18.5 138.3 %all-reduce.2.cloned.1.call-done = f32[256,3584]{1,0:T(8,128)} async-done(((f32[256,3584]{1,0:T(8,128)}), f32[256,3584]{1,0:T(8,128)}) %all-reduce.2.cloned.1.call-update) | async-done | bytes 3670032 | tf_op jit(solution)/shard_map/psum | solution.py:13
  156.7 2.5 %multiply_reduce_fusion.2 = f32[256]{0:T(256)S(1)} fusion(f32[256,3584]{1,0:T(8,128)} %all-reduce.2.cloned.1.call-done), kind=kLoop, calls=%fused_computation.9 | loop fusion | flops 1834752 | bytes 3671040 | tf_op jit(solution)/shard_map/reduce_sum | solution.py:14
  159.3 0.6 copy-done.1
  159.9 0.6 multiply_reduce_fusion.1
  160.5 2.5 %copy.13 = bf16[256,3584]{0,1:T(8,128)(2,1)} copy(bf16[256,3584]{1,0:T(8,128)(2,1)S(1)} %get-tuple-element.19) | data formatting | bytes 3670016 | tf_op jit(solution)/shard_map/convert_element_type | solution.py:15
  162.9 3.8 %all-to-all-start = ((bf16[256,8,448]{0,2,1:T(8,128)(2,1)}), bf16[256,8,448]{0,2,1:T(8,128)(2,1)S(1)}, u32[]{:S(2)}, u32[]{:S(2)}) async-start(bf16[256,8,448]{0,2,1:T(8,128)(2,1)} %bitcast.12), calls=%async_computation | async-start | bytes 3670016 | tf_op jit(solution)/shard_map/all_to_all | solution.py:33
  166.7 26.9 %all-gather = s32[8,1,256]{2,1,0:T(1,128)S(1)} all-gather(s32[1,1,256]{2,1,0:T(1,128)S(1)} %bitcast.16), channel_id=1, replica_groups=mesh['dp'=8,'mp'=4] {'dp'}, dimensions={0}, use_global_device_ids=true | all-gather | bytes 9216 | tf_op jit(solution)/shard_map/all_gather | solution.py:32
  193.6 1.0 convert_reduce_fusion
  194.6 0.0 copy-start.8
  194.6 0.2 copy.15
  194.8 1.3 copy-done.6
  196.1 3.8 %divide_convert_fusion = (bf16[1024,448]{0,1:T(8,128)(2,1)}, f32[1024,448]{0,1:T(8,128)}) fusion(f32[1024]{0:T(1024)S(1)} %multiply_add_fusion.1, bf16[2048,448]{0,1:T(8,128)(2,1)S(1)} %bitcast.13, s32[2048]{0:T(1024)S(1)} %bitcast.15, s32[1024]{0:T(1024)S(1)} %iota_add_fusion, f32[1024,448]{0,1:T(8,128)S(1)} %copy-done.6), kind=kOutput, calls=%fused_computation.10 | convolution fusion | flops 1883439104 | bytes 6438912 | tf_op jit(solution)/shard_map/while/body/eval_jaxpr/dot_general | solution.py:48
  199.9 4.7 %multiply_reduce_fusion = f32[1024]{0:T(1024)S(1)} fusion(bf16[1024,3584]{0,1:T(8,128)(2,1)} %all-gather.3.cloned.1.call-done), kind=kLoop, calls=%fused_computation | loop fusion | flops 11009024 | bytes 7344128 | tf_op jit(solution)/shard_map/reduce_sum | solution.py:24
  204.6 0.4 copy-done.2
  205.1 3.0 %fusion.6 = f32[256,1024]{1,0:T(8,128)} fusion(bf16[256,3584]{1,0:T(8,128)(2,1)S(1)} %copy-done.4, bf16[1024,3584]{0,1:T(8,128)(2,1)S(1)} %copy-done.2, f32[1024]{0:T(1024)S(1)} %multiply_reduce_fusion, f32[256]{0:T(256)S(1)} %get-tuple-element.18), kind=kOutput, calls=%fused_computation.14 | convolution fusion | flops 1879834624 | bytes 10228736 | tf_op jit(solution)/shard_map/dot_general | solution.py:20
  (18 shorter events, 0.0 us)
Async XLA Ops:
  8.0 1.0 copy-start
  8.0 148.7 %all-reduce.2.cloned.1.call-start = ((), (), s32[]{:S(2)}) async-start(), calls=%async_computation.1 | async-start | bytes 7340032 | tf_op jit(solution)/shard_map/psum | solution.py:13
  15.8 1.5 copy-start.5
  15.8 1.5 copy-start.7
  15.8 184.1 %all-gather.3.cloned.1.call-start = ((), (), s32[]{:S(2)}) async-start(), calls=%async_computation.2 | async-start | bytes 8257536 | tf_op jit(solution)/shard_map/all_gather | solution.py:19
  156.7 3.1 %copy-start.1 = (f32[256,3584]{1,0:T(8,128)S(1)}, f32[256,3584]{1,0:T(8,128)}, u32[]{:S(2)}) copy-start(f32[256,3584]{1,0:T(8,128)} %all-reduce.2.cloned.1.call-done) | copy-start | bytes 11010052
  160.5 2.5 %copy-start.3 = (bf16[256,3584]{1,0:T(8,128)(2,1)}, bf16[256,3584]{1,0:T(8,128)(2,1)S(1)}, u32[]{:S(2)}) copy-start(bf16[256,3584]{1,0:T(8,128)(2,1)S(1)} %get-tuple-element.19) | copy-start | bytes 5505028
  162.9 3.8 %copy-start.9 = (s32[256]{0:T(256)S(1)}, s32[256]{0:T(256)}, u32[]{:S(2)}) copy-start(s32[256]{0:T(256)} %param.7) | copy-start | bytes 3076
  162.9 31.6 %all-to-all-start = ((bf16[256,8,448]{0,2,1:T(8,128)(2,1)}), bf16[256,8,448]{0,2,1:T(8,128)(2,1)S(1)}, u32[]{:S(2)}, u32[]{:S(2)}) async-start(bf16[256,8,448]{0,2,1:T(8,128)(2,1)} %bitcast.12), calls=%async_computation | async-start | bytes 3670016 | tf_op jit(solution)/shard_map/all_to_all | solution.py:33
  194.6 5.3 %copy-start.8 = (f32[1024]{0:T(1024)}, f32[1024]{0:T(1024)S(1)}, u32[]{:S(2)}) copy-start(f32[1024]{0:T(1024)S(1)} %multiply_add_fusion.1) | copy-start | bytes 12292
  194.6 1.5 copy-start.6
  196.1 8.5 %copy-start.4 = (bf16[256,3584]{1,0:T(8,128)(2,1)S(1)}, bf16[256,3584]{1,0:T(8,128)(2,1)}, u32[]{:S(2)}) copy-start(bf16[256,3584]{1,0:T(8,128)(2,1)} %copy-done.3) | copy-start | bytes 5505028
  199.9 5.2 %copy-start.2 = (bf16[1024,3584]{0,1:T(8,128)(2,1)S(1)}, bf16[1024,3584]{0,1:T(8,128)(2,1)}, u32[]{:S(2)}) copy-start(bf16[1024,3584]{0,1:T(8,128)(2,1)} %all-gather.3.cloned.1.call-done) | copy-start | bytes 22020100
Sparse Core Ops, SparseCore 0:
  16.0 140.7 all-reduce.1
Sparse Core Ops, SparseCore 1:
  18.8 52.4 all-gather.2
where the time goes:
time: 216 us
  waiting for transfers between devices  138 us (64%)
  blocking collectives  26.9 us (12%)
  between operations  15.5 us (7%)
  matrix products  13.6 us (6%)
  other arithmetic  9.94 us (5%)
  local copies, waits for them, and re-layouts  7.42 us (3%)
  starting transfers between devices  3.87 us (2%)
    psum x1, waiting for transfers between devices, body(): projected = lax.psum(partial_value, 'mp')  138 us
    all_gather x1, blocking collectives, body(): every_assign = lax.all_gather(assignments, 'dp', axis=0, tiled=True)  26.9 us
    dot_general x1, matrix products, body(): partial_value = jnp.dot(pooled, w_out, preferred_element_type=jnp.float32)  6.79 us
    reduce_sum x1, other arithmetic, body(): center_norms = jnp.sum(piece_wide * piece_wide, axis=1)  4.74 us
    unnamed x20, local copies, waits for them, and re-layouts  4.72 us
  transfers between devices with their start and end apart: 3, of which 1 were waited for; matrix products, arithmetic and copies ran while one was open for 5% of the time, Pallas kernels for 0%

commit v1 on v0

--- a/solution.py
+++ b/solution.py
@@ -10,7 +10,7 @@
 
 def body(pooled, w_out, assignments, ema_sums, ema_counts):
     partial_value = jnp.dot(pooled, w_out, preferred_element_type=jnp.float32)
-    projected = lax.psum(partial_value, "mp")
+    projected = jnp.sum(lax.all_gather(partial_value, "mp"), axis=0)
     inverse_norm = 1.0 / jnp.sqrt(jnp.sum(projected * projected, axis=1, keepdims=True) + EPSILON)
     embedded = (projected * inverse_norm).astype(jnp.bfloat16)
     local_centers = ema_sums.shape[0]

time: 216 us -> 359 us (1.66)
  waiting for transfers between devices: 138 us -> 286 us
  blocking collectives: 26.9 us -> 10.4 us
  other arithmetic: 9.94 us -> 20.4 us
    all_gather x0 -> x1, waiting for transfers between devices: none -> 241 us  [body(): projected = jnp.sum(lax.all_gather(partial_value, 'mp'), axis=0)]
    psum x1 -> x0, waiting for transfers between devices: 138 us -> none  [body(): projected = lax.psum(partial_value, 'mp')]
    all_gather x1, waiting for transfers between devices: 0.01 us -> 44.4 us  [body(): column_piece = lax.all_gather(centers, 'dp', axis=1, tiled=True)]
    all_gather x1, blocking collectives: 26.9 us -> 10.4 us  [body(): every_assign = lax.all_gather(assignments, 'dp', axis=0, tiled=True)]
    reduce_sum x0 -> x1, other arithmetic: none -> 8.88 us  [body(): projected = jnp.sum(lax.all_gather(partial_value, 'mp'), axis=0)]
    reduce_sum x0 -> x1, local copies, waits for them, and re-layouts: none -> 5.33 us  [body(): projected = jnp.sum(lax.all_gather(partial_value, 'mp'), axis=0)]
  transfers between devices with their start and end apart: 3 -> 3, of which waited for: 1 -> 2; matrix products, arithmetic and copies ran while one was open for 5% -> 8% of each run, Pallas kernels for 0% -> 0%
where the time goes in v1:
time: 359 us
  waiting for transfers between devices  286 us (80%)
  other arithmetic  20.4 us (6%)
  between operations  14.1 us (4%)
  matrix products  13.6 us (4%)
  local copies, waits for them, and re-layouts  10.9 us (3%)
  blocking collectives  10.4 us (3%)
  starting transfers between devices  3.67 us (1%)
    all_gather x1, waiting for transfers between devices, body(): projected = jnp.sum(lax.all_gather(partial_value, 'mp'), axis=0)  241 us
    all_gather x1, waiting for transfers between devices, body(): column_piece = lax.all_gather(centers, 'dp', axis=1, tiled=True)  44.4 us
    all_gather x1, blocking collectives, body(): every_assign = lax.all_gather(assignments, 'dp', axis=0, tiled=True)  10.4 us
    reduce_sum x1, other arithmetic, body(): projected = jnp.sum(lax.all_gather(partial_value, 'mp'), axis=0)  8.88 us
  transfers between devices with their start and end apart: 3, of which 2 were waited for; matrix products, arithmetic and copies ran while one was open for 8% of the time, Pallas kernels for 0%

profile of v1, /device:TPU:0, one launch (start us, length us, event | category | flops | bytes accessed | tf_op | source)
XLA Modules:
  0.0 358.8 jit_solution(9337845953034196079)
XLA Ops:
  7.2 0.0 all-gather.7.cloned.1.call-start
  7.2 1.0 copy-done
  8.2 6.7 %fusion.7 = f32[256,3584]{1,0:T(8,128)} fusion(bf16[256,896]{1,0:T(8,128)(2,1)S(1)} %copy-done, bf16[896,3584]{1,0:T(8,128)(2,1)} %param.6), kind=kOutput, calls=%fused_computation.19 | convolution fusion | flops 1644167168 | bytes 10551296 | tf_op jit(solution)/shard_map/dot_general | solution.py:12
  15.0 0.0 all-gather.5.cloned.1.call-start
  15.0 1.4 copy-done.4
  16.4 1.1 divide_convert_fusion.1
  17.6 0.0 all-gather.5.cloned.1.call-update
  17.6 10.4 %all-gather.1 = s32[8,1,256]{2,1,0:T(1,128)S(1)} all-gather(s32[1,1,256]{2,1,0:T(1,128)S(1)} %bitcast.17), channel_id=1, replica_groups=mesh['dp'=8,'mp'=4] {'dp'}, dimensions={0}, use_global_device_ids=true | all-gather | bytes 9216 | tf_op jit(solution)/shard_map/all_gather | solution.py:32
  28.0 1.0 convert_reduce_fusion
  29.0 241.3 %all-gather.7.cloned.1.call-done = f32[1024,3584]{1,0:T(8,128)} async-done(((f32[256,3584]{1,0:T(8,128)}), f32[1024,3584]{1,0:T(8,128)}) %all-gather.7.cloned.1.call-update) | async-done | bytes 14680080 | tf_op jit(solution)/shard_map/all_gather | solution.py:13
  270.3 8.9 %reduce_sum.48 = f32[256,3584]{1,0:T(8,128)} reduce(f32[4,256,3584]{2,1,0:T(8,128)} %bitcast.12, f32[]{:T(128)} %constant.7.clone.1), dimensions={0}, to_apply=%region_0.0 | reduce | flops 2752512 | bytes 18350084 | tf_op jit(solution)/shard_map/reduce_sum | solution.py:13
  279.2 5.3 %copy.12 = f32[256,3584]{0,1:T(8,128)} copy(f32[256,3584]{1,0:T(8,128)} %reduce_sum.48) | data formatting | bytes 7340032 | tf_op jit(solution)/shard_map/reduce_sum | solution.py:13
  284.5 2.5 multiply_reduce_fusion.2
  287.0 0.6 copy-done.2
  287.7 1.6 multiply_convert_fusion
  289.3 3.6 %all-to-all-start = ((bf16[256,8,448]{0,2,1:T(8,128)(2,1)}), bf16[256,8,448]{0,2,1:T(8,128)(2,1)S(1)}, u32[]{:S(2)}, u32[]{:S(2)}) async-start(bf16[256,8,448]{0,2,1:T(8,128)(2,1)} %multiply_convert_fusion), calls=%async_computation | async-start | bytes 3670016 | tf_op jit(solution)/shard_map/all_to_all | solution.py:33
  292.9 44.4 %all-gather.5.cloned.1.call-done = bf16[1024,3584]{0,1:T(8,128)(2,1)} async-done(((bf16[1024,448]{0,1:T(8,128)(2,1)}), bf16[1024,3584]{0,1:T(8,128)(2,1)}) %all-gather.5.cloned.1.call-update) | async-done | bytes 7340048 | tf_op jit(solution)/shard_map/all_gather | solution.py:19
  337.3 4.7 %multiply_reduce_fusion = f32[1024]{0:T(1024)S(1)} fusion(bf16[1024,3584]{0,1:T(8,128)(2,1)} %all-gather.5.cloned.1.call-done), kind=kLoop, calls=%fused_computation | loop fusion | flops 11009024 | bytes 7344128 | tf_op jit(solution)/shard_map/reduce_sum | solution.py:24
  342.0 0.5 multiply_reduce_fusion.1
  342.5 1.0 copy-done.3
  343.5 3.1 fusion.6
  346.6 0.2 copy.14
  346.9 1.3 copy-done.5
  348.1 3.8 %divide_convert_fusion = (bf16[1024,448]{0,1:T(8,128)(2,1)}, f32[1024,448]{0,1:T(8,128)}) fusion(f32[1024]{0:T(1024)S(1)} %multiply_add_fusion.1, bf16[2048,448]{0,1:T(8,128)(2,1)S(1)} %bitcast.14, s32[2048]{0:T(1024)S(1)} %bitcast.16, s32[1024]{0:T(1024)S(1)} %iota_add_fusion, f32[1024,448]{0,1:T(8,128)S(1)} %copy-done.5), kind=kOutput, calls=%fused_computation.11 | convolution fusion | flops 1883439104 | bytes 6438912 | tf_op jit(solution)/shard_map/while/body/eval_jaxpr/dot_general | solution.py:48
  (18 shorter events, 0.1 us)
Async XLA Ops:
  7.2 1.0 copy-start
  7.2 263.1 %all-gather.7.cloned.1.call-start = ((), (), s32[]{:S(2)}) async-start(), calls=%async_computation.2 | async-start | bytes 18350080 | tf_op jit(solution)/shard_map/all_gather | solution.py:13
  14.9 1.5 copy-start.4
  14.9 1.5 copy-start.6
  14.9 2.7 copy-start.8
  15.0 322.3 %all-gather.5.cloned.1.call-start = ((), (), s32[]{:S(2)}) async-start(), calls=%async_computation.1 | async-start | bytes 8257536 | tf_op jit(solution)/shard_map/all_gather | solution.py:19
  29.0 317.9 %copy-start.7 = (f32[1024]{0:T(1024)}, f32[1024]{0:T(1024)S(1)}, u32[]{:S(2)}) copy-start(f32[1024]{0:T(1024)S(1)} %multiply_add_fusion.1) | copy-start | bytes 12292
  284.5 3.1 copy-start.2
  289.3 57.4 %all-to-all-start = ((bf16[256,8,448]{0,2,1:T(8,128)(2,1)}), bf16[256,8,448]{0,2,1:T(8,128)(2,1)S(1)}, u32[]{:S(2)}, u32[]{:S(2)}) async-start(bf16[256,8,448]{0,2,1:T(8,128)(2,1)} %multiply_convert_fusion), calls=%async_computation | async-start | bytes 3670016 | tf_op jit(solution)/shard_map/all_to_all | solution.py:33
  337.3 4.7 %copy-start.1 = (f32[256,3584]{1,0:T(8,128)S(1)}, f32[256,3584]{1,0:T(8,128)}, u32[]{:S(2)}) copy-start(f32[256,3584]{1,0:T(8,128)} %reduce_sum.48) | copy-start | bytes 11010052
  337.3 6.3 %copy-start.3 = (bf16[1024,3584]{0,1:T(8,128)(2,1)S(1)}, bf16[1024,3584]{0,1:T(8,128)(2,1)}, u32[]{:S(2)}) copy-start(bf16[1024,3584]{0,1:T(8,128)(2,1)} %all-gather.5.cloned.1.call-done) | copy-start | bytes 22020100
  346.6 1.5 copy-start.5
Sparse Core Ops, SparseCore 0:
  15.1 255.1 all-gather.6
  272.8 64.4 all-gather.4
